TPU v7x, 32 devices: a whole 2x2x4 slice. The times are simulated.
32 devices in a mesh: gx: 8 (over z, x), gy: 4 (over y, core).
Axes of the slice: x: 2, y: 2, z: 4, core: 2. Of those that a mesh axis runs over, the one named last changes fastest.
Arguments:
- voxels: bfloat16 [64, 32, 8, 96], P('gx', 'gy'), may hold values from -6 to 6
- occupancy: int32 [64, 32, 8], P('gx', 'gy'), may hold values 0 or 1
- conv_weight: bfloat16 [27, 96, 96], replicated, may hold values from -0.125 to 0.125
- conv_bias: float32 [96], replicated, may hold values from -3 to 3
- down_weight: bfloat16 [27, 96, 96], replicated, may hold values from -0.125 to 0.125
- down_cotangent: bfloat16 [32, 16, 4, 96], P('gx', 'gy'), may hold values from -6 to 6
Outputs:
- down: bfloat16 [32, 16, 4, 96], P('gx', 'gy')
- grad_voxels: bfloat16 [64, 32, 8, 96], P('gx', 'gy')
- grad_conv: float32 [27, 96, 96], replicated
- grad_bias: float32 [96], replicated
- grad_down: float32 [27, 96, 96], replicated
Inputs may be any that keep to these rules, and one draw needn't show every extreme that they name: `occupancy`: 0 or 1 for every voxel.
All inputs are finite; a program needn't handle non-finite values. No bound on the sum of `occupancy` on one device may be relied on, other than what follows from the above.
Results may differ from a plain program's by a relative error of at most 0.006.
Values may be sent and summed in bfloat16 or wider, within the bound.
No kernel may reach another device: no remote copies, remote signals or barrier semaphores. Data moves between devices by JAX's collectives and lax.ppermute only.
A program may use at most 64 MiB of HBM per device.

v0:
```python
import functools
import math

import jax
import jax.numpy as jnp
from jax import lax
from jax.experimental import pallas as pl
from jax.experimental.pallas import tpu as pltpu
from jax.sharding import Mesh
from jax.sharding import PartitionSpec as P


LANES = 128
F32 = jnp.float32
BF16 = jnp.bfloat16
NT = (((1,), (1,)), ((), ()))
TN = (((0,), (0,)), ((), ()))
MIB = 1024 * 1024


def call(body, outs, args, scratch=(), cost=None, vmem=8, far=(), far_outs=False, sems=0):
    near_spec = pl.BlockSpec(memory_space=pltpu.VMEM)
    far_spec = pl.BlockSpec(memory_space=pltpu.HBM)
    args = [
        pltpu.with_memory_space_constraint(a, pltpu.HBM) if i in far else a
        for i, a in enumerate(args)
    ]
    return pl.pallas_call(
        body,
        out_shape=tuple(jax.ShapeDtypeStruct(s, d) for s, d in outs),
        in_specs=[far_spec if i in far else near_spec for i in range(len(args))],
        out_specs=tuple(far_spec if far_outs else near_spec for _ in outs),
        scratch_shapes=[pltpu.VMEM(s, d) for s, d in scratch]
        + ([pltpu.SemaphoreType.DMA((sems,))] if sems else []),
        compiler_params=pltpu.CompilerParams(vmem_limit_bytes=vmem * MIB),
        cost_estimate=cost,
    )(*args)


def fetch(pairs, sems):
    copies = [pltpu.make_async_copy(a, b, sems.at[i]) for i, (a, b) in enumerate(pairs)]
    for copy in copies:
        copy.start()
    for copy in copies:
        copy.wait()


def lane_of(shape):
    return lax.broadcasted_iota(jnp.int32, shape, len(shape) - 1)


def z_of(shape):
    return lax.broadcasted_iota(jnp.int32, shape, len(shape) - 2)


def below(v):
    return jnp.where(z_of(v.shape) == 0, 0.0, pltpu.roll(v, 1, axis=1))


def above(v):
    top = v.shape[1] - 1
    return jnp.where(z_of(v.shape) == top, 0.0, pltpu.roll(v, top, axis=1))


def first_kernel(
    dims, vox_far, occ_far, cot_far, x_ref, u_ref, core_ref, side_ref,
    xs, us, vox_ref, occ_ref, cot_ref, sems,
):
    tx, ty, tz, ch = dims
    fetch(((vox_far, vox_ref), (occ_far, occ_ref), (cot_far, cot_ref)), sems)
    hx, hy = tx // 2, ty // 2
    occ = jnp.broadcast_to(occ_ref[...].astype(F32)[:, :, None], (tx * ty, tz, LANES))
    xs[...] = jnp.zeros(xs.shape, F32)
    xs[:, :ch] = vox_ref[...].astype(F32)
    x = xs[...].reshape(tx * ty, tz, LANES)
    x = jnp.where(lane_of(x.shape) == ch, 1.0, x) * occ
    xs[...] = x.reshape(xs.shape)
    x_ref[...] = xs[...].astype(BF16)
    pairs = occ.reshape(hx, 2, hy, 2, tz, LANES)
    pairs = jnp.maximum(pairs[:, 0], pairs[:, 1])
    pairs = jnp.maximum(pairs[:, :, 0], pairs[:, :, 1]).reshape(hx * hy, tz, LANES)
    coarse = jnp.maximum(pairs, pltpu.roll(pairs, tz - 1, axis=1))
    us[...] = jnp.zeros(us.shape, F32)
    cot = jnp.concatenate(
        [cot_ref[...].astype(F32), jnp.zeros((hx * hy * tz // 2, LANES - ch), F32)], axis=1
    )
    us[pl.ds(0, hx * hy * tz // 2, stride=2), :] = cot
    u = us[...].reshape(hx * hy, tz, LANES)
    even = lax.rem(z_of(u.shape), 2) == 0
    u = jnp.where((lane_of(u.shape) == ch) & even, 1.0, u) * coarse
    us[...] = u.reshape(us.shape)
    u_ref[...] = us[...].astype(BF16)
    core = lax.axis_index("core")
    x4, u4 = xs.reshape(tx, ty, tz, LANES), us.reshape(hx, hy, tz, LANES)
    rows = tx * 2 * tz
    for ref, low in ((core_ref, core), (side_ref, 1 - core)):
        start = (1 - low) * (ty - 2)
        ref[:rows] = x4[:, pl.ds(start, 2)].reshape(rows, LANES).astype(BF16)
        ref[rows:] = (
            u4[:, pl.ds((1 - low) * (hy - 1), 1)].reshape(hx * tz, LANES).astype(BF16)
        )


def second_kernel(dims, x_ref, u_ref, core_ref, side_ref, near_ref, far_ref, xe, ue):
    tx, ty, tz, _ = dims
    widen(dims, x_ref, u_ref, core_ref, side_ref, xe, ue, 0, 0)
    odd = lax.rem(lax.axis_index("gx"), 2)
    rows = 2 * (ty + 4) * tz
    hx, hy = tx // 2, ty // 2
    for ref, low in ((near_ref, odd), (far_ref, 1 - odd)):
        ref[:rows] = xe[pl.ds((1 - low) * (tx - 2), 2)].reshape(rows, LANES).astype(BF16)
        ref[rows:] = (
            ue[pl.ds((1 - low) * (hx - 1), 1)].reshape((hy + 2) * tz, LANES).astype(BF16)
        )


def widen(dims, x_ref, u_ref, core_ref, side_ref, xe, ue, x0, u0):
    tx, ty, tz, _ = dims
    hx, hy = tx // 2, ty // 2
    rows = tx * 2 * tz
    core = lax.axis_index("core")
    xe[x0 : x0 + tx, 2 : 2 + ty] = x_ref[...].astype(F32).reshape(tx, ty, tz, LANES)
    ue[u0 : u0 + hx, 1 : 1 + hy] = u_ref[...].astype(F32).reshape(hx, hy, tz, LANES)
    inside = in_grid(1 - core, "gyc")
    for ref, low, real in ((core_ref, core, True), (side_ref, 1 - core, inside)):
        part = jnp.where(real, ref[...].astype(F32), 0.0)
        xe[x0 : x0 + tx, pl.ds((1 - low) * (ty + 2), 2)] = part[:rows].reshape(tx, 2, tz, LANES)
        ue[u0 : u0 + hx, pl.ds((1 - low) * (hy + 1), 1)] = part[rows:].reshape(hx, 1, tz, LANES)


def in_grid(low, axis):
    me = lax.axis_index(axis)
    return jnp.where(low == 1, me > 0, me < lax.axis_size(axis) - 1)


def taps_in_rows(ch, w_ref, out):
    out[...] = jnp.zeros(out.shape, BF16)
    for t in range(w_ref.shape[0]):
        out[t // 3, (t % 3) * LANES : (t % 3) * LANES + ch, :ch] = w_ref[t]


def taps_in_lanes(ch, w_ref, out):
    out[...] = jnp.zeros(out.shape, BF16)
    for t in range(w_ref.shape[0]):
        at, lane = t // 3 * LANES, t % 3 * LANES
        out[at : at + ch, lane : lane + ch] = w_ref[t]


def weights_kernel(ch, cw_far, dw_far, bias_far, cl_ref, dr_ref, b_ref, cw, dw, bias, sems):
    fetch(((cw_far, cw), (dw_far, dw), (bias_far, bias)), sems)
    taps_in_lanes(ch, cw, cl_ref)
    taps_in_rows(ch, dw, dr_ref)
    b_ref[...] = jnp.zeros(b_ref.shape, F32)
    b_ref[:, :ch] = bias[...]


def other_weights_kernel(ch, cw, dw, cr_ref, dl_ref):
    taps_in_rows(ch, cw, cr_ref)
    taps_in_lanes(ch, dw, dl_ref)


def three(v):
    return v[:, :, :LANES], v[:, :, LANES : 2 * LANES], v[:, :, 2 * LANES :]


def pack_block(block, ch):
    free = LANES - ch
    keep = ch * ch // LANES
    tail = block[keep:ch]
    parts = [
        pltpu.roll(tail, (LANES - free - p * free) % LANES, axis=1) for p in range(ch // free)
    ]
    parts = jnp.concatenate(parts, axis=0)
    main = block[:keep]
    return jnp.where(lane_of(main.shape) < ch, main, parts)


def unpack_block(packed, ch):
    free = LANES - ch
    keep = ch * ch // LANES
    tall = ch - keep
    lane = lane_of((tall, LANES))
    tail = None
    for p in range(ch // free):
        part = packed[p * tall : (p + 1) * tall]
        part = pltpu.roll(part, (free + p * free) % LANES, axis=1)
        tail = part if tail is None else jnp.where(lane < p * free, tail, part)
    return jnp.concatenate([packed, tail], axis=0)


def fine_gradient(rows, wd, picks):
    wins = [win.reshape(rows, LANES).astype(BF16) for _, win, _ in picks]
    taps = [wd[a * 3 + b] for a, _, b in picks]
    return lax.dot_general(
        jnp.concatenate(wins, axis=1), jnp.concatenate(taps, axis=1), NT,
        preferred_element_type=F32,
    )


def z_sum(out, lower, upper):
    low, same, high = three(out)
    return lower(low) + same + upper(high)


def unit(v, bias, x, g, ch):
    v = v + bias[...].reshape(1, 1, LANES)
    live = jnp.broadcast_to(x[:, :, ch : ch + 1], x.shape)
    s = 1.0 / (1.0 + jnp.exp(-v))
    summed = (x + live * (v * s)).astype(BF16).astype(F32)
    grad = (g * live * s * (1.0 + v * (1.0 - s))).astype(BF16).astype(F32)
    return summed, grad


def with_ones(win, a, b, ch):
    if a == 1 and b == 1:
        win = jnp.where(lane_of(win.shape) == ch + 1, 1.0, win)
    return win


def z_taps(other):
    cells = other.shape[0] * other.shape[1]
    other = jnp.concatenate([above(other), other, below(other)], axis=2)
    return other.reshape(cells, 3 * LANES).astype(BF16)


TERMS = {0: ((2, 0), (0, 1)), 1: ((1, 1),)}


def inner_kernel(
    dims, x_ref, u_ref, core_ref, side_ref, wf, wd, bias, gp_ref, s_ref, gs_ref, acc_ref,
    xe, ue, pre, gsr, gp,
):
    tx, ty, tz, ch = dims
    hx, hy = tx // 2, ty // 2
    ey, inner = ty + 2, tx - 2
    widen(dims, x_ref, u_ref, core_ref, side_ref, xe, ue, 0, 0)
    wins = [
        xe[a : a + inner, b : b + ey].reshape(inner * ey * tz, LANES).astype(BF16)
        for a in range(3)
        for b in range(3)
    ]
    out = jnp.dot(jnp.concatenate(wins, axis=1), wf[...], preferred_element_type=F32)
    out = z_sum(out.reshape(inner * ey, tz, 3 * LANES), below, above)
    pre[...] = out.reshape(inner, ey, tz, LANES)
    for px in (0, 1):
        for py in (0, 1):
            picks = [
                (a, ue[sx : sx + hx - 1, sy : sy + hy + 1], b)
                for a, sx in TERMS[px]
                for b, sy in TERMS[py]
            ]
            out = fine_gradient((hx - 1) * (hy + 1) * tz, wd, picks)
            out = z_sum(out.reshape((hx - 1) * (hy + 1), tz, 3 * LANES), above, below)
            gsr[:, px, :, py] = out.reshape(hx - 1, hy + 1, tz, LANES)

    def pointwise(i, _):
        g = gsr[i // 2, lax.rem(i, 2)].reshape(ey, tz, LANES)
        summed, grad = unit(pre[i], bias, xe[i + 1, 1 : 1 + ey], g, ch)
        at = pl.ds(pl.multiple_of(i * ey * tz, 16), ey * tz)
        s_ref[at] = summed.reshape(ey * tz, LANES).astype(BF16)
        gp_ref[at] = grad.reshape(ey * tz, LANES).astype(BF16)
        gp[i] = grad
        return 0

    lax.fori_loop(0, inner, pointwise, 0)
    gs_ref[...] = gsr[...].reshape(inner, ey, tz, LANES)[:, 1 : 1 + ty].reshape(
        inner * ty * tz, LANES
    )
    other = z_taps(gp[:, 1 : 1 + ty].reshape(inner * ty, tz, LANES))
    for a in range(3):
        wins = [
            with_ones(xe[a : a + inner, b + 1 : b + 1 + ty], a, b, ch)
            .reshape(inner * ty * tz, LANES)
            .astype(BF16)
            for b in range(3)
        ]
        acc_ref[a * 3 * LANES : (a + 1) * 3 * LANES] = lax.dot_general(
            jnp.concatenate(wins, axis=1), other, TN, preferred_element_type=F32
        )


def main_kernel(
    dims, x_ref, u_ref, core_ref, side_ref, near_ref, far_ref, wf, wd, bias, gpa_ref, sa_ref, acc_ref,
    send_ref, gpb_ref, sb_ref, gsb_ref, win_ref, other_ref,
    xe, ue, ss, pre, gsr, edge, pack,
):
    tx, ty, tz, ch = dims
    hx, hy = tx // 2, ty // 2
    ex, ey = tx + 2, ty + 2
    slab = ey * tz
    core = lax.axis_index("core")
    odd = lax.rem(lax.axis_index("gx"), 2)
    widen(dims, x_ref, u_ref, core_ref, side_ref, xe, ue, 2, 1)
    rows = 2 * (ty + 4) * tz
    inside = in_grid(1 - odd, "gx")
    for ref, low, real in ((near_ref, odd, True), (far_ref, 1 - odd, inside)):
        part = jnp.where(real, ref[...].astype(F32), 0.0)
        xe[pl.ds((1 - low) * (tx + 2), 2)] = part[:rows].reshape(2, ty + 4, tz, LANES)
        ue[pl.ds((1 - low) * (hx + 1), 1)] = part[rows:].reshape(1, hy + 2, tz, LANES)
    ss[1:hx] = sa_ref[...].astype(F32).reshape(hx - 1, 2, hy + 1, 2, tz, LANES)

    def edges(v, a, lower, upper):
        return jnp.concatenate([v[lower + a : lower + a + 2], v[upper + a : upper + a + 2]], axis=0)

    wins = [
        edges(xe, a, 0, ex - 2)[:, b : b + ey].reshape(4 * slab, LANES).astype(BF16)
        for a in range(3)
        for b in range(3)
    ]
    out = jnp.dot(jnp.concatenate(wins, axis=1), wf[...], preferred_element_type=F32)
    out = z_sum(out.reshape(4 * ey, tz, 3 * LANES), below, above)
    pre[...] = out.reshape(4, ey, tz, LANES)
    for px in (0, 1):
        for py in (0, 1):
            picks = []
            for a, sx in TERMS[px]:
                for b, sy in TERMS[py]:
                    win = jnp.concatenate(
                        [ue[sx, sy : sy + hy + 1], ue[hx + sx, sy : sy + hy + 1]], axis=0
                    )
                    picks.append((a, win, b))
            out = fine_gradient(2 * (hy + 1) * tz, wd, picks)
            out = z_sum(out.reshape(2 * (hy + 1), tz, 3 * LANES), above, below)
            gsr[:, px, :, py] = out.reshape(2, hy + 1, tz, LANES)
    for j, i in enumerate((0, 1, ex - 2, ex - 1)):
        g = gsr[j // 2, j % 2].reshape(ey, tz, LANES)
        summed, grad = unit(pre[j], bias, xe[i + 1, 1 : 1 + ey], g, ch)
        ss[i // 2, i % 2] = summed.reshape(hy + 1, 2, tz, LANES)
        sb_ref[j * slab : (j + 1) * slab] = summed.reshape(slab, LANES).astype(BF16)
        gpb_ref[j * slab : (j + 1) * slab] = grad.reshape(slab, LANES).astype(BF16)
        if j in (1, 2):
            edge[j - 1] = grad[1 : 1 + ty]
            gsb_ref[(j - 1) * ty * tz : j * ty * tz] = g[1 : 1 + ty].reshape(ty * tz, LANES)

    def fine_window(a, b):
        win = jnp.concatenate(
            [xe[a + 1, b + 1 : b + 1 + ty], xe[tx + a, b + 1 : b + 1 + ty]], axis=0
        )
        return with_ones(win, a, b, ch).reshape(2 * ty * tz, LANES).astype(BF16)

    def coarse_window(a, b):
        win = ss[a // 2 : a // 2 + hx, a % 2, b // 2 : b // 2 + hy, b % 2]
        return win.reshape(hx * hy * tz, LANES).astype(BF16)

    own = ue[1 : 1 + hx, 1 : 1 + hy].reshape(hx * hy, tz, LANES)
    for h, window, other in (
        (0, fine_window, z_taps(edge[...].reshape(2 * ty, tz, LANES))),
        (1, coarse_window, z_taps(own)),
    ):
        rows = other.shape[0]
        for ab in range(9):
            win_ref[h, :rows, ab * LANES : (ab + 1) * LANES] = window(ab // 3, ab % 3)
        other_ref[h, :rows] = other
        if rows < win_ref.shape[1]:
            win_ref[h, rows:] = jnp.zeros((win_ref.shape[1] - rows, win_ref.shape[2]), BF16)
            other_ref[h, rows:] = jnp.zeros((win_ref.shape[1] - rows, 3 * LANES), BF16)
    half_gradients(ch, 1 - core, win_ref, other_ref, acc_ref, pack)
    send_ref[...] = pack[...].astype(BF16)


def half_gradients(ch, h, win_ref, other_ref, acc_ref, pack):
    block_rows = ch * ch // LANES
    for a in range(3):
        part = slice(a * 3 * LANES, (a + 1) * 3 * LANES)
        out = lax.dot_general(win_ref[h, :, part], other_ref[h], TN, preferred_element_type=F32)
        out = out + jnp.where(h == 0, acc_ref[part], 0.0)
        for b in range(3):
            for e in range(3):
                at = (a * 9 + b * 3 + e) * block_rows
                block = out[b * LANES : b * LANES + ch, e * LANES : (e + 1) * LANES]
                pack[at : at + block_rows] = pack_block(block, ch)
        if a == 1:
            at = 27 * block_rows
            pack[at : at + 8] = out[LANES + ch : LANES + ch + 8, LANES : 2 * LANES]
    at = 27 * block_rows + 8
    pack[at:] = jnp.zeros((pack.shape[0] - at, LANES), F32)


def keep_kernel(ch, win_ref, other_ref, acc_ref, keep_ref):
    half_gradients(ch, lax.axis_index("core"), win_ref, other_ref, acc_ref, keep_ref)


def second_outputs(
    dims, x_ref, u_ref, gpa_ref, gpb_ref, gsa_ref, gsb_ref, sa_ref, sb_ref, wf, wd, down_ref, gv_ref,
    ge, ss, accd,
):
    tx, ty, tz, ch = dims
    hx, hy = tx // 2, ty // 2
    ex, ey = tx + 2, ty + 2
    slab = ey * tz
    ge[2:tx] = gpa_ref[...].astype(F32).reshape(tx - 2, ey, tz, LANES)
    ss[1:hx] = sa_ref[...].astype(F32).reshape(hx - 1, 2, hy + 1, 2, tz, LANES)
    for j, i in enumerate((0, 1, ex - 2, ex - 1)):
        ge[i] = gpb_ref[j * slab : (j + 1) * slab].astype(F32).reshape(ey, tz, LANES)
        ss[i // 2, i % 2] = (
            sb_ref[j * slab : (j + 1) * slab].astype(F32).reshape(hy + 1, 2, tz, LANES)
        )
    wins = [
        ss[a // 2 : a // 2 + hx, a % 2, b // 2 : b // 2 + hy, b % 2]
        .reshape(hx * hy * tz, LANES)
        .astype(BF16)
        for a in range(3)
        for b in range(3)
    ]
    out = jnp.dot(jnp.concatenate(wins, axis=1), wd[...], preferred_element_type=F32)
    out = z_sum(out.reshape(hx * hy, tz, 3 * LANES), below, above).reshape(hx * hy * tz, LANES)
    u = u_ref[...].astype(F32)
    accd[...] = out * jnp.broadcast_to(u[:, ch : ch + 1], u.shape)
    down_ref[...] = accd[pl.ds(0, hx * hy * tz // 2, stride=2), :][:, :ch].astype(BF16)

    wins = [
        ge[2 - a : 2 - a + tx, 2 - b : 2 - b + ty].reshape(tx * ty * tz, LANES).astype(BF16)
        for a in range(3)
        for b in range(3)
    ]
    taps = jnp.concatenate([wf[ab] for ab in range(9)], axis=1)
    out = lax.dot_general(jnp.concatenate(wins, axis=1), taps, NT, preferred_element_type=F32)
    out = z_sum(out.reshape(tx * ty, tz, 3 * LANES), above, below).reshape(tx * ty * tz, LANES)
    x = x_ref[...].astype(F32)
    live = jnp.broadcast_to(x[:, ch : ch + 1], x.shape)
    column = ty * tz
    grad = jnp.concatenate([gsb_ref[:column], gsa_ref[...], gsb_ref[column:]], axis=0)
    gv_ref[...] = ((grad + out) * live)[:, :ch].astype(BF16)


def peers_of(core):
    return 0, 1 + core, 2 - core, 3


def split_kernel(keep_ref, got_ref, own_ref, *to_refs):
    me = lax.rem(lax.axis_index("gx"), 2) * 2 + lax.rem(lax.axis_index("gyc"), 2)
    rows = own_ref.shape[0]
    for k, ref in zip(peers_of(lax.axis_index("core")), (own_ref, *to_refs)):
        at = pl.ds(pl.multiple_of((me ^ k) * rows, 16), rows)
        ref[...] = (keep_ref[at] + got_ref[at].astype(F32)).astype(ref.dtype)


def sum_kernel(own_ref, a_ref, b_ref, c_ref, out_ref):
    out_ref[...] = (
        own_ref[...] + a_ref[...].astype(F32) + b_ref[...].astype(F32) + c_ref[...].astype(F32)
    ).astype(BF16)


def unpacked_half(ch, factor, half, parts, full, out, bias):
    me = lax.rem(lax.axis_index("gx"), 2) * 2 + lax.rem(lax.axis_index("gyc"), 2)
    rows = parts[0].shape[0]
    block_rows = ch * ch // LANES
    for k, part in zip(peers_of(half), parts):
        at = pl.ds(pl.multiple_of((me ^ k) * rows, 16), rows)
        full[at] = part[...].astype(F32) * factor
    bias[...] = full[27 * block_rows + 1 : 27 * block_rows + 2]
    for t in range(27):
        out[t] = unpack_block(full[t * block_rows : (t + 1) * block_rows], ch)[:, :ch]
        yield t


def own_kernel(ch, factor, *refs):
    parts, (out, bias, full) = refs[:4], refs[4:]
    for _ in unpacked_half(ch, factor, lax.axis_index("core"), parts, full, out, bias):
        pass


def last_kernel(ch, factor, *refs):
    parts, (own, own_bias, conv_ref, down_ref, bias_ref, full, out, bias, bias_out, sems) = (
        refs[:4], refs[4:],
    )
    core = lax.axis_index("core")

    def moves(src, part, sem, first):
        for c, ref in ((0, conv_ref), (1, down_ref)):
            yield (core == c) == first, pltpu.make_async_copy(src.at[part], ref.at[part], sem)

    every = [(own, pl.ds(0, 27), sems.at[0], True)]
    every += [(out, pl.ds(a * 9, 9), sems.at[1 + a], False) for a in range(3)]

    def start(n):
        for wanted, copy in moves(*every[n]):
            pl.when(wanted)(copy.start)

    start(0)
    for t in unpacked_half(ch, factor, 1 - core, parts, full, out, bias):
        if t % 9 == 8:
            start(1 + t // 9)
    bias_out[...] = jnp.where(core == 0, own_bias[...], bias[...])[:, :ch]
    last = pltpu.make_async_copy(bias_out, bias_ref, sems.at[4])
    last.start()
    for move in every:
        for wanted, copy in moves(*move):
            pl.when(wanted)(copy.wait)
    last.wait()


def on_device(voxels, occupancy, conv_weight, conv_bias, down_weight, down_cotangent):
    tx, ty, tz, ch = voxels.shape
    hx, hy, hz = tx // 2, ty // 2, tz // 2
    ex, ey = tx + 2, ty + 2
    dims = (tx, ty, tz, ch)
    n_gx, n_gyc = lax.axis_size("gx"), lax.axis_size("gyc")
    fine, coarse = tx * ty * tz, hx * hy * tz

    side_rows = tx * 2 * tz + hx * tz
    row_rows = 2 * (ty + 4) * tz + (hy + 2) * tz
    x, u, to_core, to_side = call(
        functools.partial(first_kernel, dims),
        [((fine, LANES), BF16), ((coarse, LANES), BF16)] + [((side_rows, LANES), BF16)] * 2,
        (
            voxels.reshape(fine, ch),
            occupancy.reshape(tx * ty, tz),
            down_cotangent.reshape(hx * hy * hz, ch),
        ),
        [
            ((fine, LANES), F32),
            ((coarse, LANES), F32),
            ((fine, ch), BF16),
            ((tx * ty, tz), jnp.int32),
            ((hx * hy * hz, ch), BF16),
        ],
        vmem=4,
        far=(0, 1, 2),
        sems=3,
    )
    swap = [(0, 1), (1, 0)]
    n_gy = n_gyc * 2
    sides = [(i, (i + (1 if i % 2 else -1)) % n_gy) for i in range(n_gy)]
    from_core = lax.ppermute(to_core, "core", swap)
    from_side = lax.ppermute(to_side, ("gyc", "core"), sides)
    in_lanes, in_rows = ((9 * LANES, 3 * LANES), BF16), ((9, 3 * LANES, LANES), BF16)
    weights = call(
        functools.partial(weights_kernel, ch),
        [in_lanes, in_rows, ((1, LANES), F32), ((27, ch, ch), BF16), ((27, ch, ch), BF16)],
        (conv_weight, down_weight, conv_bias.reshape(1, ch)),
        [((1, ch), F32)],
        vmem=4,
        far=(0, 1, 2),
        sems=3,
    )
    from_core, from_side, *weights = lax.optimization_barrier((from_core, from_side, *weights))
    conv_lanes, down_rows, bias, raw_conv, raw_down = weights
    to_near, to_far = call(
        functools.partial(second_kernel, dims),
        [((row_rows, LANES), BF16)] * 2,
        (x, u, from_core, from_side),
        [((tx, ty + 4, tz, LANES), F32), ((hx, hy + 2, tz, LANES), F32)],
        vmem=4,
    )
    near = [(i, i ^ 1) for i in range(n_gx)]
    far = []
    for i in range(n_gx):
        peer = i + (1 if i % 2 else -1)
        for j in range(n_gy):
            to = i * n_gy + (j ^ 1) if peer in (-1, n_gx) else peer * n_gy + j
            far.append((i * n_gy + j, to))
    from_near = lax.ppermute(to_near, "gx", near)
    from_far = lax.ppermute(to_far, ("gx", "gyc", "core"), far)
    inner = tx - 2
    *results, = call(
        functools.partial(inner_kernel, dims),
        [((inner * ey * tz, LANES), BF16)] * 2
        + [((inner * ty * tz, LANES), F32), ((9 * LANES, 3 * LANES), F32)],
        (x, u, from_core, from_side, conv_lanes, down_rows, bias),
        [
            ((tx, ty + 4, tz, LANES), F32),
            ((hx, hy + 2, tz, LANES), F32),
            ((inner, ey, tz, LANES), F32),
            ((hx - 1, 2, hy + 1, 2, tz, LANES), F32),
            ((inner, ey, tz, LANES), F32),
        ],
        cost=pl.CostEstimate(flops=5_000_000_000, bytes_accessed=4_000_000, transcendentals=0),
        vmem=12,
    )
    from_far, from_near, *results = lax.optimization_barrier((from_far, from_near, *results))
    gp_inner, s_inner, gs_inner, acc = results

    block_rows = ch * ch // LANES
    half_rows = -(-(27 * block_rows + 8) // 64) * 64
    cells = max(2 * ty * tz, coarse)
    send, gp_edge, s_edge, gs_edge, wins, others = call(
        functools.partial(main_kernel, dims),
        [((half_rows, LANES), BF16)]
        + [((4 * ey * tz, LANES), BF16)] * 2
        + [((2 * ty * tz, LANES), F32)]
        + [((2, cells, 9 * LANES), BF16), ((2, cells, 3 * LANES), BF16)],
        (
            x, u, from_core, from_side, from_near, from_far, conv_lanes, down_rows, bias,
            gp_inner, s_inner, acc,
        ),
        [
            ((tx + 4, ty + 4, tz, LANES), F32),
            ((hx + 2, hy + 2, tz, LANES), F32),
            ((hx + 1, 2, hy + 1, 2, tz, LANES), F32),
            ((4, ey, tz, LANES), F32),
            ((2, 2, hy + 1, 2, tz, LANES), F32),
            ((2, ty, tz, LANES), F32),
            ((half_rows, LANES), F32),
        ],
        vmem=12,
    )
    got = lax.ppermute(send, "core", swap)
    (keep,) = call(
        functools.partial(keep_kernel, ch),
        [((half_rows, LANES), F32)],
        (wins, others, acc),
        cost=pl.CostEstimate(flops=2_000_000_000, bytes_accessed=4_000_000, transcendentals=0),
        vmem=6,
    )
    got, keep = lax.optimization_barrier((got, keep))

    rest = call(
        functools.partial(other_weights_kernel, ch),
        [in_rows, in_lanes],
        (raw_conv, raw_down),
        vmem=4,
    )
    conv_rows, down_lanes = rest
    down, grad_voxels = call(
        functools.partial(second_outputs, dims),
        [((hx * hy * hz, ch), BF16), ((fine, ch), BF16)],
        (x, u, gp_inner, gp_edge, gs_inner, gs_edge, s_inner, s_edge, conv_rows, down_lanes),
        [
            ((ex, ey, tz, LANES), F32),
            ((hx + 1, 2, hy + 1, 2, tz, LANES), F32),
            ((coarse, LANES), F32),
        ],
        cost=pl.CostEstimate(flops=5_000_000_000, bytes_accessed=4_000_000, transcendentals=0),
        vmem=12,
    )

    def plus(a, b):
        return (a.astype(F32) + b.astype(F32)).astype(BF16)

    quarter = half_rows // 4
    mine, *pieces = call(
        split_kernel,
        [((quarter, LANES), F32)] + [((quarter, LANES), BF16)] * 3,
        (keep, got),
        vmem=2,
    )

    def across(value, turn):
        route = []
        for i in range(n_gx):
            for j in range(n_gyc):
                for c in range(2):
                    k = peers_of(c)[turn]
                    peer = (i ^ (k >> 1)) * n_gyc + (j ^ (k & 1))
                    route.append(((i * n_gyc + j) * 2 + c, peer * 2 + c))
        return lax.ppermute(value, ("gx", "gyc", "core"), route)

    arrived = [across(piece, k) for k, piece in zip((1, 2, 3), pieces)]
    *arrived, down, grad_voxels = lax.optimization_barrier((*arrived, down, grad_voxels))
    (total,) = call(sum_kernel, [((quarter, LANES), BF16)], (mine, *arrived), vmem=2)
    steps = []
    for place, peers in ((0, n_gx), (1, n_gyc)):
        step = 2
        while step < peers:
            steps.append((step, 0) if place == 0 else (0, step))
            step *= 2
    for one, two in zip(steps, steps[::-1]):
        route = []
        for i in range(n_gx):
            for j in range(n_gyc):
                for c, (dx, dy) in enumerate((one, two)):
                    at = ((i * n_gyc + j) * 2 + c, ((i ^ dx) * n_gyc + (j ^ dy)) * 2 + c)
                    route.append(at)
        total = plus(total, lax.ppermute(total, ("gx", "gyc", "core"), route))
    own = [total] + [across(total, k) for k in (1, 2, 3)]
    other = []
    for piece in own:
        other.append(lax.ppermute(piece, "core", swap))
    factor = 1.0 / math.sqrt(tx * n_gx * ty * n_gy * tz)
    whole = [((27, ch, ch), F32), ((1, LANES), F32)]
    mine = call(
        functools.partial(own_kernel, ch, factor),
        whole,
        own,
        [((half_rows, LANES), F32)],
        cost=pl.CostEstimate(flops=1_000_000_000, bytes_accessed=4_000_000, transcendentals=0),
        vmem=4,
    )
    other[1], *mine = lax.optimization_barrier((other[1], *mine))
    grad_conv, grad_down, grad_bias = call(
        functools.partial(last_kernel, ch, factor),
        [((27, ch, ch), F32), ((27, ch, ch), F32), ((1, ch), F32)],
        (*other, *mine),
        [((half_rows, LANES), F32)] + whole + [((1, ch), F32)],
        vmem=8,
        far_outs=True,
        sems=5,
    )
    return (
        down.reshape(hx, hy, hz, ch),
        grad_voxels.reshape(tx, ty, tz, ch),
        grad_conv,
        grad_bias.reshape(ch),
        grad_down,
    )


def solution(mesh):
    n_gx, n_gy = mesh.shape["gx"], mesh.shape["gy"]
    split = Mesh(mesh.devices.reshape(n_gx, n_gy // 2, 2), ("gx", "gyc", "core"))
    gy = ("gyc", "core")
    placed = (
        P("gx", gy, None, None),
        P("gx", gy, None),
        P(),
        P(),
        P(),
        P("gx", gy, None, None),
    )

    return jax.shard_map(
        on_device,
        mesh=split,
        in_specs=placed,
        out_specs=(P("gx", gy, None, None), P("gx", gy, None, None), P(), P(), P()),
        check_vma=False,
    )
```

profile of v0, /device:TPU:0, one launch (start us, length us, event | category | flops | bytes accessed | tf_op | source)
XLA Modules:
  0.0 49.0 jit_solution(3342176929222972477)
XLA Ops:
  0.6 1.1 %shard_map.101 = (bf16[512,128]{1,0:T(8,128)(2,1)S(1)}, bf16[128,128]{1,0:T(8,128)(2,1)S(1)}, bf16[160,128]{1,0:T(8,128)(2,1)S(1)}, bf16[160,128]{1,0:T(8,128)(2,1)S(1)}) custom-call(bf16[512,96]{1,0:T(8,128)(2,1)} %bitcast.7, s32[64,8]{1,0:T(8,128)} %bitcast.8, bf16[64,96]{1,0:T(8,128)(2,1)} %bitcast.9), custom_call_target="tpu_custom_call" | custom-call | tf_op jit(solution)/shard_map/pallas_call | solution.py:28
  1.7 0.6 %collective-permute-start = (bf16[160,128]{1,0:T(8,128)(2,1)S(1)}, bf16[160,128]{1,0:T(8,128)(2,1)S(1)}, u32[]{:S(2)}, u32[]{:S(2)}) collective-permute-start(bf16[160,128]{1,0:T(8,128)(2,1)S(1)} %get-tuple-element.64), channel_id=1, source_target_pairs={{0,1},{1,0},{2,3},{3,2},{4,5},{5,4},{6,7},{7,6},{8,9},{9,8},{10,11... | collective-permute-start | bytes 122888 | tf_op jit(solution)/shard_map/ppermute | solution.py:525
  2.3 2.6 %collective-permute-start.1 = (bf16[160,128]{1,0:T(8,128)(2,1)S(1)}, bf16[160,128]{1,0:T(8,128)(2,1)S(1)}, u32[]{:S(2)}, u32[]{:S(2)}) collective-permute-start(bf16[160,128]{1,0:T(8,128)(2,1)S(1)} %get-tuple-element.65), channel_id=1, source_target_pairs={{0,3},{1,2},{2,1},{3,0},{4,7},{5,6},{6,5},{7,4},{8,11},{9,10},{10,... | collective-permute-start | bytes 122888 | tf_op jit(solution)/shard_map/ppermute | solution.py:526
  4.9 1.7 %shard_map.102 = (bf16[1152,384]{1,0:T(8,128)(2,1)S(1)}, bf16[9,384,128]{2,1,0:T(8,128)(2,1)S(1)}, f32[1,128]{1,0:T(1,128)S(1)}, bf16[27,96,96]{2,1,0:T(8,128)(2,1)S(1)}, bf16[27,96,96]{2,1,0:T(8,128)(2,1)S(1)}) custom-call(bf16[27,96,96]{2,1,0:T(8,128)(2,1)} %cw_far.1, bf16[27,96,96]{2,1,0:T(8,128)(2,1)} %dw_far.1, f32[1,96]{1,0:T(1,128)} %bitcast.10), custom_call_target="tpu_custom_call" | custom-call | tf_op jit(solution)/shard_map/pallas_call | solution.py:28
  6.6 0.0 collective-permute-done.core_ref
  6.6 0.1 collective-permute-done.1.side_ref
  6.8 0.1 shard_map.103
  6.8 0.2 collective-permute-start.2
  7.0 2.9 %collective-permute-start.3 = (bf16[240,128]{1,0:T(8,128)(2,1)S(1)}, bf16[240,128]{1,0:T(8,128)(2,1)S(1)}, u32[]{:S(2)}, u32[]{:S(2)}) collective-permute-start(bf16[240,128]{1,0:T(8,128)(2,1)S(1)} %get-tuple-element.74), channel_id=1, source_target_pairs={{0,4},{4,0},{8,12},{12,8},{16,20},{20,16},{24,28},{28,24},{1,5},{5... | collective-permute-start | bytes 184328 | tf_op jit(solution)/shard_map/ppermute | solution.py:553
  9.9 2.3 %shard_map.104 = (bf16[480,128]{1,0:T(8,128)(2,1)S(1)}, bf16[480,128]{1,0:T(8,128)(2,1)S(1)}, f32[384,128]{1,0:T(8,128)S(1)}, f32[1152,384]{1,0:T(8,128)S(1)}) custom-call(bf16[512,128]{1,0:T(8,128)(2,1)S(1)} %get-tuple-element.62.x_ref, bf16[128,128]{1,0:T(8,128)(2,1)S(1)} %get-tuple-element.63.u_ref, bf16[160,128]{1,0:T(8,128)(2,1)S(1)} %collective-permute-done.core_ref, ...), custom_call_target="tpu_custom_call" | custom-call | flops 5000000000 | bytes 4000000 | tf_op jit(solution)/shard_map/pallas_call | solution.py:28
  12.2 0.0 collective-permute-done.2.far_ref
  12.2 0.2 collective-permute-done.3.near_ref
  12.5 1.3 %shard_map.105 = (bf16[1984,128]{1,0:T(8,128)(2,1)S(1)}, bf16[320,128]{1,0:T(8,128)(2,1)S(1)}, bf16[320,128]{1,0:T(8,128)(2,1)S(1)}, f32[128,128]{1,0:T(8,128)S(...) custom-call(bf16[512,128]{1,0:T(8,128)(2,1)S(1)} %get-tuple-element.62.x_ref, ...), custom_call_target="tpu_custom_call" | custom-call | tf_op jit(solution)/shard_map/pallas_call | solution.py:28
  13.8 0.1 collective-permute-start.4
  13.9 0.4 shard_map.108
  14.3 0.6 %shard_map.106.keep_ref = f32[1984,128]{1,0:T(8,128)S(1)} custom-call(bf16[2,128,1152]{2,1,0:T(8,128)(2,1)S(1)} %get-tuple-element.88.win_ref, bf16[2,128,384]{2,1,0:T(8,128)(2,1)S(1)} %get-tuple-element.89.other_ref, f32[1152,384]{1,0:T(8,128)S(1)} %get-tuple-element.86.acc_ref), custom_call_target="tpu_custom_call" | custom-call | flops 2000000000 | bytes 4000000 | tf_op jit(solution)/shard_map/pallas_call | solution.py:28
  14.9 0.9 %collective-permute-done.4.got_ref = bf16[1984,128]{1,0:T(8,128)(2,1)S(1)} collective-permute-done((bf16[1984,128]{1,0:T(8,128)(2,1)S(1)}, bf16[1984,128]{1,0:T(8,128)(2,1)S(1)}, u32[]{:S(2)}, u32[]{:S(2)}) %collective-permute-start.4) | collective-permute-done | bytes 507936 | tf_op jit(solution)/shard_map/ppermute | solution.py:598
  15.8 0.1 shard_map.107
  15.9 1.6 %collective-permute-start.5 = (bf16[496,128]{1,0:T(8,128)(2,1)S(1)}, bf16[496,128]{1,0:T(8,128)(2,1)S(1)}, u32[]{:S(2)}, u32[]{:S(2)}) collective-permute-start(bf16[496,128]{1,0:T(8,128)(2,1)S(1)} %get-tuple-element.92), channel_id=1, source_target_pairs={{0,2},{1,5},{2,0},{3,7},{4,6},{5,1},{6,4},{7,3},{8,10},{9,13},{10,... | collective-permute-start | bytes 380936 | tf_op jit(solution)/shard_map/ppermute | solution.py:647
  17.5 2.5 %collective-permute-start.6 = (bf16[496,128]{1,0:T(8,128)(2,1)S(1)}, bf16[496,128]{1,0:T(8,128)(2,1)S(1)}, u32[]{:S(2)}, u32[]{:S(2)}) collective-permute-start(bf16[496,128]{1,0:T(8,128)(2,1)S(1)} %get-tuple-element.93), channel_id=1, source_target_pairs={{0,4},{1,3},{2,6},{3,1},{4,0},{5,7},{6,2},{7,5},{8,12},{9,11},{10,... | collective-permute-start | bytes 380936 | tf_op jit(solution)/shard_map/ppermute | solution.py:647
  19.9 0.0 collective-permute-start.7
  19.9 1.7 %shard_map.109 = (bf16[64,96]{1,0:T(8,128)(2,1)}, bf16[512,96]{1,0:T(8,128)(2,1)}) custom-call(bf16[512,128]{1,0:T(8,128)(2,1)S(1)} %get-tuple-element.62.x_ref, bf16[128,128]{1,0:T(8,128)(2,1)S(1)} %get-tuple-element.63.u_ref, bf16[480,128]{1,0:T(8,128)(2,1)S(1)} %get-tuple-element.84.gpa_ref, bf16[320,128]{1,0:T(8,128)(2,1)S(1)} %get-tuple-element.95.gpb_ref, ...), custom_call_target="tpu_custom_call" | custom-call | flops 5000000000 | bytes 4000000 | tf_op jit(solution)/shard_map/pallas_call | solution.py:28
  21.6 0.0 collective-permute-done.5.a_ref
  21.6 2.0 %collective-permute-done.6.b_ref = bf16[496,128]{1,0:T(8,128)(2,1)S(1)} collective-permute-done((bf16[496,128]{1,0:T(8,128)(2,1)S(1)}, bf16[496,128]{1,0:T(8,128)(2,1)S(1)}, u32[]{:S(2)}, u32[]{:S(2)}) %collective-permute-start.6) | collective-permute-done | bytes 127008 | tf_op jit(solution)/shard_map/ppermute | solution.py:647
  23.6 2.2 %collective-permute-done.7.c_ref = bf16[496,128]{1,0:T(8,128)(2,1)S(1)} collective-permute-done((bf16[496,128]{1,0:T(8,128)(2,1)S(1)}, bf16[496,128]{1,0:T(8,128)(2,1)S(1)}, u32[]{:S(2)}, u32[]{:S(2)}) %collective-permute-start.7) | collective-permute-done | bytes 127008 | tf_op jit(solution)/shard_map/ppermute | solution.py:647
  25.8 0.1 shard_map.110
  25.9 1.9 %collective-permute-start.8 = (bf16[496,128]{1,0:T(8,128)(2,1)S(1)}, bf16[496,128]{1,0:T(8,128)(2,1)S(1)}, u32[]{:S(2)}, u32[]{:S(2)}) collective-permute-start(bf16[496,128]{1,0:T(8,128)(2,1)S(1)} %shard_map.110), channel_id=1, source_target_pairs={{0,8},{1,17},{2,10},{3,19},{4,12},{5,21},{6,14},{7,23},{8,0},{9,25... | collective-permute-start | bytes 380936 | tf_op jit(solution)/shard_map/ppermute | solution.py:665
  27.8 3.4 %collective-permute-done.8 = bf16[496,128]{1,0:T(8,128)(2,1)S(1)} collective-permute-done((bf16[496,128]{1,0:T(8,128)(2,1)S(1)}, bf16[496,128]{1,0:T(8,128)(2,1)S(1)}, u32[]{:S(2)}, u32[]{:S(2)}) %collective-permute-start.8) | collective-permute-done | bytes 127008 | tf_op jit(solution)/shard_map/ppermute | solution.py:665
  31.2 2.7 %collective-permute-start.9 = (bf16[496,128]{1,0:T(8,128)(2,1)S(1)}, bf16[496,128]{1,0:T(8,128)(2,1)S(1)}, u32[]{:S(2)}, u32[]{:S(2)}) collective-permute-start(bf16[496,128]{1,0:T(8,128)(2,1)S(1)} %add_convert_fusion.1), channel_id=1, source_target_pairs={{0,16},{1,9},{2,18},{3,11},{4,20},{5,13},{6,22},{7,15},{8,24},{9,1... | collective-permute-start | bytes 380936 | tf_op jit(solution)/shard_map/ppermute | solution.py:665
  34.0 3.1 %collective-permute-done.9 = bf16[496,128]{1,0:T(8,128)(2,1)S(1)} collective-permute-done((bf16[496,128]{1,0:T(8,128)(2,1)S(1)}, bf16[496,128]{1,0:T(8,128)(2,1)S(1)}, u32[]{:S(2)}, u32[]{:S(2)}) %collective-permute-start.9) | collective-permute-done | bytes 127008 | tf_op jit(solution)/shard_map/ppermute | solution.py:665
  37.2 1.3 %collective-permute-start.11 = (bf16[496,128]{1,0:T(8,128)(2,1)S(1)}, bf16[496,128]{1,0:T(8,128)(2,1)S(1)}, u32[]{:S(2)}, u32[]{:S(2)}) collective-permute-start(bf16[496,128]{1,0:T(8,128)(2,1)S(1)} %add_convert_fusion.refs_0_), channel_id=1, source_target_pairs={{0,2},{1,5},{2,0},{3,7},{4,6},{5,1},{6,4},{7,3},{8,10},{9,13},{10,... | collective-permute-start | bytes 380936 | tf_op jit(solution)/shard_map/ppermute | solution.py:647
  38.5 1.8 %collective-permute-start.13 = (bf16[496,128]{1,0:T(8,128)(2,1)S(1)}, bf16[496,128]{1,0:T(8,128)(2,1)S(1)}, u32[]{:S(2)}, u32[]{:S(2)}) collective-permute-start(bf16[496,128]{1,0:T(8,128)(2,1)S(1)} %add_convert_fusion.refs_0_), channel_id=1, source_target_pairs={{0,4},{1,3},{2,6},{3,1},{4,0},{5,7},{6,2},{7,5},{8,12},{9,11},{10,... | collective-permute-start | bytes 380936 | tf_op jit(solution)/shard_map/ppermute | solution.py:647
  40.3 1.4 %collective-permute-start.14 = (bf16[496,128]{1,0:T(8,128)(2,1)S(1)}, bf16[496,128]{1,0:T(8,128)(2,1)S(1)}, u32[]{:S(2)}, u32[]{:S(2)}) collective-permute-start(bf16[496,128]{1,0:T(8,128)(2,1)S(1)} %add_convert_fusion.refs_0_), channel_id=1, source_target_pairs={{0,6},{1,7},{2,4},{3,5},{4,2},{5,3},{6,0},{7,1},{8,14},{9,15},{10,... | collective-permute-start | bytes 380936 | tf_op jit(solution)/shard_map/ppermute | solution.py:647
  41.7 1.3 %collective-permute-done.11.refs_1_ = bf16[496,128]{1,0:T(8,128)(2,1)S(1)} collective-permute-done((bf16[496,128]{1,0:T(8,128)(2,1)S(1)}, bf16[496,128]{1,0:T(8,128)(2,1)S(1)}, u32[]{:S(2)}, u32[]{:S(2)}) %collective-permute-start.11) | collective-permute-done | bytes 127008 | tf_op jit(solution)/shard_map/ppermute | solution.py:647
  43.0 0.0 collective-permute-start.12
  43.0 0.5 %collective-permute-start.10 = (bf16[496,128]{1,0:T(8,128)(2,1)S(1)}, bf16[496,128]{1,0:T(8,128)(2,1)S(1)}, u32[]{:S(2)}, u32[]{:S(2)}) collective-permute-start(bf16[496,128]{1,0:T(8,128)(2,1)S(1)} %add_convert_fusion.refs_0_), channel_id=1, source_target_pairs={{0,1},{1,0},{2,3},{3,2},{4,5},{5,4},{6,7},{7,6},{8,9},{9,8},{10,11... | collective-permute-start | bytes 380936 | tf_op jit(solution)/shard_map/ppermute | solution.py:669
  43.5 0.0 collective-permute-done.13.refs_2_
  43.5 0.0 collective-permute-start.15
  43.5 2.6 %collective-permute-done.14.refs_3_ = bf16[496,128]{1,0:T(8,128)(2,1)S(1)} collective-permute-done((bf16[496,128]{1,0:T(8,128)(2,1)S(1)}, bf16[496,128]{1,0:T(8,128)(2,1)S(1)}, u32[]{:S(2)}, u32[]{:S(2)}) %collective-permute-start.14) | collective-permute-done | bytes 127008 | tf_op jit(solution)/shard_map/ppermute | solution.py:647
  46.1 0.0 collective-permute-start.16
  46.1 0.4 shard_map.111
  46.5 0.0 collective-permute-done.12.refs_1_
  46.5 0.0 collective-permute-done.10.refs_0_
  46.5 0.0 collective-permute-done.15.refs_2_
  46.5 0.9 %collective-permute-done.16.refs_3_ = bf16[496,128]{1,0:T(8,128)(2,1)S(1)} collective-permute-done((bf16[496,128]{1,0:T(8,128)(2,1)S(1)}, bf16[496,128]{1,0:T(8,128)(2,1)S(1)}, u32[]{:S(2)}, u32[]{:S(2)}) %collective-permute-start.16) | collective-permute-done | bytes 127008 | tf_op jit(solution)/shard_map/ppermute | solution.py:669
  47.4 1.6 %shard_map.112 = (f32[27,96,96]{2,1,0:T(8,128)}, f32[27,96,96]{2,1,0:T(8,128)}, f32[1,96]{1,0:T(1,128)}) custom-call(bf16[496,128]{1,0:T(8,128)(2,1)S(1)} %collective-permute-done.10.refs_0_, bf16[496,128]{1,0:T(8,128)(2,1)S(1)} %collective-permute-done.12.refs_1_, bf16[496,128]{1,0:T(8,128)(2,1)S(1)} %collective-permute-done.15.refs_2_, ...), custom_call_target="tpu_custom_call" | custom-call | tf_op jit(solution)/shard_map/pallas_call | solution.py:28
  (2 shorter events, 0.1 us)
Async XLA Ops:
  1.7 4.9 %collective-permute-start = (bf16[160,128]{1,0:T(8,128)(2,1)S(1)}, bf16[160,128]{1,0:T(8,128)(2,1)S(1)}, u32[]{:S(2)}, u32[]{:S(2)}) collective-permute-start(bf16[160,128]{1,0:T(8,128)(2,1)S(1)} %get-tuple-element.64), channel_id=1, source_target_pairs={{0,1},{1,0},{2,3},{3,2},{4,5},{5,4},{6,7},{7,6},{8,9},{9,8},{10,11... | collective-permute-start | bytes 122888 | tf_op jit(solution)/shard_map/ppermute | solution.py:525
  2.3 4.5 %collective-permute-start.1 = (bf16[160,128]{1,0:T(8,128)(2,1)S(1)}, bf16[160,128]{1,0:T(8,128)(2,1)S(1)}, u32[]{:S(2)}, u32[]{:S(2)}) collective-permute-start(bf16[160,128]{1,0:T(8,128)(2,1)S(1)} %get-tuple-element.65), channel_id=1, source_target_pairs={{0,3},{1,2},{2,1},{3,0},{4,7},{5,6},{6,5},{7,4},{8,11},{9,10},{10,... | collective-permute-start | bytes 122888 | tf_op jit(solution)/shard_map/ppermute | solution.py:526
  6.8 5.4 %collective-permute-start.2 = (bf16[240,128]{1,0:T(8,128)(2,1)S(1)}, bf16[240,128]{1,0:T(8,128)(2,1)S(1)}, u32[]{:S(2)}, u32[]{:S(2)}) collective-permute-start(bf16[240,128]{1,0:T(8,128)(2,1)S(1)} %get-tuple-element.73), channel_id=1, source_target_pairs={{0,1},{1,0},{2,3},{3,2},{4,8},{5,9},{6,10},{7,11},{8,4},{9,5},{10,... | collective-permute-start | bytes 184328 | tf_op jit(solution)/shard_map/ppermute | solution.py:554
  7.0 5.5 %collective-permute-start.3 = (bf16[240,128]{1,0:T(8,128)(2,1)S(1)}, bf16[240,128]{1,0:T(8,128)(2,1)S(1)}, u32[]{:S(2)}, u32[]{:S(2)}) collective-permute-start(bf16[240,128]{1,0:T(8,128)(2,1)S(1)} %get-tuple-element.74), channel_id=1, source_target_pairs={{0,4},{4,0},{8,12},{12,8},{16,20},{20,16},{24,28},{28,24},{1,5},{5... | collective-permute-start | bytes 184328 | tf_op jit(solution)/shard_map/ppermute | solution.py:553
  13.8 2.0 %collective-permute-start.4 = (bf16[1984,128]{1,0:T(8,128)(2,1)S(1)}, bf16[1984,128]{1,0:T(8,128)(2,1)S(1)}, u32[]{:S(2)}, u32[]{:S(2)}) collective-permute-start(bf16[1984,128]{1,0:T(8,128)(2,1)S(1)} %get-tuple-element.87), channel_id=1, source_target_pairs={{0,1},{1,0},{2,3},{3,2},{4,5},{5,4},{6,7},{7,6},{8,9},{9,8},{10,11... | collective-permute-start | bytes 1523720 | tf_op jit(solution)/shard_map/ppermute | solution.py:598
  15.9 5.7 %collective-permute-start.5 = (bf16[496,128]{1,0:T(8,128)(2,1)S(1)}, bf16[496,128]{1,0:T(8,128)(2,1)S(1)}, u32[]{:S(2)}, u32[]{:S(2)}) collective-permute-start(bf16[496,128]{1,0:T(8,128)(2,1)S(1)} %get-tuple-element.92), channel_id=1, source_target_pairs={{0,2},{1,5},{2,0},{3,7},{4,6},{5,1},{6,4},{7,3},{8,10},{9,13},{10,... | collective-permute-start | bytes 380936 | tf_op jit(solution)/shard_map/ppermute | solution.py:647
  17.5 6.2 %collective-permute-start.6 = (bf16[496,128]{1,0:T(8,128)(2,1)S(1)}, bf16[496,128]{1,0:T(8,128)(2,1)S(1)}, u32[]{:S(2)}, u32[]{:S(2)}) collective-permute-start(bf16[496,128]{1,0:T(8,128)(2,1)S(1)} %get-tuple-element.93), channel_id=1, source_target_pairs={{0,4},{1,3},{2,6},{3,1},{4,0},{5,7},{6,2},{7,5},{8,12},{9,11},{10,... | collective-permute-start | bytes 380936 | tf_op jit(solution)/shard_map/ppermute | solution.py:647
  19.9 5.9 %collective-permute-start.7 = (bf16[496,128]{1,0:T(8,128)(2,1)S(1)}, bf16[496,128]{1,0:T(8,128)(2,1)S(1)}, u32[]{:S(2)}, u32[]{:S(2)}) collective-permute-start(bf16[496,128]{1,0:T(8,128)(2,1)S(1)} %get-tuple-element.94), channel_id=1, source_target_pairs={{0,6},{1,7},{2,4},{3,5},{4,2},{5,3},{6,0},{7,1},{8,14},{9,15},{10,... | collective-permute-start | bytes 380936 | tf_op jit(solution)/shard_map/ppermute | solution.py:647
  25.9 5.3 %collective-permute-start.8 = (bf16[496,128]{1,0:T(8,128)(2,1)S(1)}, bf16[496,128]{1,0:T(8,128)(2,1)S(1)}, u32[]{:S(2)}, u32[]{:S(2)}) collective-permute-start(bf16[496,128]{1,0:T(8,128)(2,1)S(1)} %shard_map.110), channel_id=1, source_target_pairs={{0,8},{1,17},{2,10},{3,19},{4,12},{5,21},{6,14},{7,23},{8,0},{9,25... | collective-permute-start | bytes 380936 | tf_op jit(solution)/shard_map/ppermute | solution.py:665
  31.2 5.9 %collective-permute-start.9 = (bf16[496,128]{1,0:T(8,128)(2,1)S(1)}, bf16[496,128]{1,0:T(8,128)(2,1)S(1)}, u32[]{:S(2)}, u32[]{:S(2)}) collective-permute-start(bf16[496,128]{1,0:T(8,128)(2,1)S(1)} %add_convert_fusion.1), channel_id=1, source_target_pairs={{0,16},{1,9},{2,18},{3,11},{4,20},{5,13},{6,22},{7,15},{8,24},{9,1... | collective-permute-start | bytes 380936 | tf_op jit(solution)/shard_map/ppermute | solution.py:665
  37.2 5.8 %collective-permute-start.11 = (bf16[496,128]{1,0:T(8,128)(2,1)S(1)}, bf16[496,128]{1,0:T(8,128)(2,1)S(1)}, u32[]{:S(2)}, u32[]{:S(2)}) collective-permute-start(bf16[496,128]{1,0:T(8,128)(2,1)S(1)} %add_convert_fusion.refs_0_), channel_id=1, source_target_pairs={{0,2},{1,5},{2,0},{3,7},{4,6},{5,1},{6,4},{7,3},{8,10},{9,13},{10,... | collective-permute-start | bytes 380936 | tf_op jit(solution)/shard_map/ppermute | solution.py:647
  38.5 5.0 %collective-permute-start.13 = (bf16[496,128]{1,0:T(8,128)(2,1)S(1)}, bf16[496,128]{1,0:T(8,128)(2,1)S(1)}, u32[]{:S(2)}, u32[]{:S(2)}) collective-permute-start(bf16[496,128]{1,0:T(8,128)(2,1)S(1)} %add_convert_fusion.refs_0_), channel_id=1, source_target_pairs={{0,4},{1,3},{2,6},{3,1},{4,0},{5,7},{6,2},{7,5},{8,12},{9,11},{10,... | collective-permute-start | bytes 380936 | tf_op jit(solution)/shard_map/ppermute | solution.py:647
  40.3 5.8 %collective-permute-start.14 = (bf16[496,128]{1,0:T(8,128)(2,1)S(1)}, bf16[496,128]{1,0:T(8,128)(2,1)S(1)}, u32[]{:S(2)}, u32[]{:S(2)}) collective-permute-start(bf16[496,128]{1,0:T(8,128)(2,1)S(1)} %add_convert_fusion.refs_0_), channel_id=1, source_target_pairs={{0,6},{1,7},{2,4},{3,5},{4,2},{5,3},{6,0},{7,1},{8,14},{9,15},{10,... | collective-permute-start | bytes 380936 | tf_op jit(solution)/shard_map/ppermute | solution.py:647
  43.0 3.5 %collective-permute-start.12 = (bf16[496,128]{1,0:T(8,128)(2,1)S(1)}, bf16[496,128]{1,0:T(8,128)(2,1)S(1)}, u32[]{:S(2)}, u32[]{:S(2)}) collective-permute-start(bf16[496,128]{1,0:T(8,128)(2,1)S(1)} %collective-permute-done.11.refs_1_), channel_id=1, source_target_pairs={{0,1},{1,0},{2,3},{3,2},{4,5},{5,4},{6,7},{7,6},{8,9},{9,8},{10,11... | collective-permute-start | bytes 380936 | tf_op jit(solution)/shard_map/ppermute | solution.py:669
  43.0 3.5 %collective-permute-start.10 = (bf16[496,128]{1,0:T(8,128)(2,1)S(1)}, bf16[496,128]{1,0:T(8,128)(2,1)S(1)}, u32[]{:S(2)}, u32[]{:S(2)}) collective-permute-start(bf16[496,128]{1,0:T(8,128)(2,1)S(1)} %add_convert_fusion.refs_0_), channel_id=1, source_target_pairs={{0,1},{1,0},{2,3},{3,2},{4,5},{5,4},{6,7},{7,6},{8,9},{9,8},{10,11... | collective-permute-start | bytes 380936 | tf_op jit(solution)/shard_map/ppermute | solution.py:669
  43.5 3.0 %collective-permute-start.15 = (bf16[496,128]{1,0:T(8,128)(2,1)S(1)}, bf16[496,128]{1,0:T(8,128)(2,1)S(1)}, u32[]{:S(2)}, u32[]{:S(2)}) collective-permute-start(bf16[496,128]{1,0:T(8,128)(2,1)S(1)} %collective-permute-done.13.refs_2_), channel_id=1, source_target_pairs={{0,1},{1,0},{2,3},{3,2},{4,5},{5,4},{6,7},{7,6},{8,9},{9,8},{10,11... | collective-permute-start | bytes 380936 | tf_op jit(solution)/shard_map/ppermute | solution.py:669
  46.1 1.3 %collective-permute-start.16 = (bf16[496,128]{1,0:T(8,128)(2,1)S(1)}, bf16[496,128]{1,0:T(8,128)(2,1)S(1)}, u32[]{:S(2)}, u32[]{:S(2)}) collective-permute-start(bf16[496,128]{1,0:T(8,128)(2,1)S(1)} %collective-permute-done.14.refs_3_), channel_id=1, source_target_pairs={{0,1},{1,0},{2,3},{3,2},{4,5},{5,4},{6,7},{7,6},{8,9},{9,8},{10,11... | collective-permute-start | bytes 380936 | tf_op jit(solution)/shard_map/ppermute | solution.py:669
where the time goes:
time: 49.2 us; the launch traced here: 49 us
  starting transfers between devices  20.1 us (41%)
  waiting for transfers between devices  16.8 us (34%)
  Pallas kernels  11.3 us (23%)
  between operations  0.75 us (2%)
    pallas_call x12, Pallas kernels, call(): pl.pallas_call(body, out_shape=tuple((jax.ShapeDtypeStruct(s, d) for s, d...  11.3 us
    ppermute x6, starting transfers between devices, across(): return lax.ppermute(value, ('gx', 'gyc', 'core'), route)  8.54 us
    ppermute x6, waiting for transfers between devices, across(): return lax.ppermute(value, ('gx', 'gyc', 'core'), route)  8.09 us
    ppermute x2, waiting for transfers between devices, on_device(): total = plus(total, lax.ppermute(total, ('gx', 'gyc', 'core'), route))  6.58 us
    ppermute x2, starting transfers between devices, on_device(): total = plus(total, lax.ppermute(total, ('gx', 'gyc', 'core'), route))  4.64 us
    ppermute x1, starting transfers between devices, on_device(): from_near = lax.ppermute(to_near, 'gx', near)  2.94 us
    ppermute x1, starting transfers between devices, on_device(): from_side = lax.ppermute(to_side, ('gyc', 'core'), sides)  2.62 us
  transfers between devices with their start and end apart: 17, of which 10 were waited for; matrix products, arithmetic and copies ran while one was open for 0% of the time, Pallas kernels for 14%

commit v1 on v0

--- a/solution.py
+++ b/solution.py
@@ -521,9 +521,14 @@
     )
     swap = [(0, 1), (1, 0)]
     n_gy = n_gyc * 2
-    sides = [(i, (i + (1 if i % 2 else -1)) % n_gy) for i in range(n_gy)]
+    sides = []
+    for i in range(n_gx):
+        for j in range(n_gy):
+            peer = j + (1 if j % 2 else -1)
+            to = (i ^ 1) * n_gy + j if peer in (-1, n_gy) else i * n_gy + peer
+            sides.append((i * n_gy + j, to))
     from_core = lax.ppermute(to_core, "core", swap)
-    from_side = lax.ppermute(to_side, ("gyc", "core"), sides)
+    from_side = lax.ppermute(to_side, ("gx", "gyc", "core"), sides)
     in_lanes, in_rows = ((9 * LANES, 3 * LANES), BF16), ((9, 3 * LANES, LANES), BF16)
     weights = call(
         functools.partial(weights_kernel, ch),

time: 49.2 us -> 49.9 us (1.014)
  waiting for transfers between devices: 16.8 us -> 18 us
  starting transfers between devices: 20.1 us -> 19.5 us
    ppermute x6, starting transfers between devices: 8.54 us -> 7.64 us  [across(): return lax.ppermute(value, ('gx', 'gyc', 'core'), route)]
    ppermute x6, waiting for transfers between devices: 8.09 us -> 8.88 us  [across(): return lax.ppermute(value, ('gx', 'gyc', 'core'), route)]
    ppermute x2, waiting for transfers between devices: 6.58 us -> 7.12 us  [on_device(): total = plus(total, lax.ppermute(total, ('gx', 'gyc', 'core'), route))]
    ppermute x1, starting transfers between devices: 2.94 us -> 3.45 us  [on_device(): from_near = lax.ppermute(to_near, 'gx', near)]
where the time goes in v1:
time: 49.9 us; the launch traced here: 49.7 us
  starting transfers between devices  19.5 us (39%)
  waiting for transfers between devices  18 us (36%)
  Pallas kernels  11.3 us (23%)
  between operations  0.76 us (2%)
    pallas_call x12, Pallas kernels, call(): pl.pallas_call(body, out_shape=tuple((jax.ShapeDtypeStruct(s, d) for s, d...  11.3 us
    ppermute x6, waiting for transfers between devices, across(): return lax.ppermute(value, ('gx', 'gyc', 'core'), route)  8.88 us
    ppermute x6, starting transfers between devices, across(): return lax.ppermute(value, ('gx', 'gyc', 'core'), route)  7.64 us
    ppermute x2, waiting for transfers between devices, on_device(): total = plus(total, lax.ppermute(total, ('gx', 'gyc', 'core'), route))  7.12 us
    ppermute x2, starting transfers between devices, on_device(): total = plus(total, lax.ppermute(total, ('gx', 'gyc', 'core'), route))  4.57 us
    ppermute x1, starting transfers between devices, on_device(): from_near = lax.ppermute(to_near, 'gx', near)  3.45 us
    ppermute x1, starting transfers between devices, on_device(): from_side = lax.ppermute(to_side, ('gx', 'gyc', 'core'), sides)  2.55 us
  transfers between devices with their start and end apart: 17, of which 10 were waited for; matrix products, arithmetic and copies ran while one was open for 0% of the time, Pallas kernels for 14%

profile of v1, /device:TPU:0, one launch (start us, length us, event | category | flops | bytes accessed | tf_op | source)
XLA Modules:
  0.0 49.7 jit_solution(11421873816596765540)
XLA Ops:
  0.6 1.1 %shard_map.101 = (bf16[512,128]{1,0:T(8,128)(2,1)S(1)}, bf16[128,128]{1,0:T(8,128)(2,1)S(1)}, bf16[160,128]{1,0:T(8,128)(2,1)S(1)}, bf16[160,128]{1,0:T(8,128)(2,1)S(1)}) custom-call(bf16[512,96]{1,0:T(8,128)(2,1)} %bitcast.7, s32[64,8]{1,0:T(8,128)} %bitcast.8, bf16[64,96]{1,0:T(8,128)(2,1)} %bitcast.9), custom_call_target="tpu_custom_call" | custom-call | tf_op jit(solution)/shard_map/pallas_call | solution.py:28
  1.7 0.6 %collective-permute-start = (bf16[160,128]{1,0:T(8,128)(2,1)S(1)}, bf16[160,128]{1,0:T(8,128)(2,1)S(1)}, u32[]{:S(2)}, u32[]{:S(2)}) collective-permute-start(bf16[160,128]{1,0:T(8,128)(2,1)S(1)} %get-tuple-element.64), channel_id=1, source_target_pairs={{0,1},{1,0},{2,3},{3,2},{4,5},{5,4},{6,7},{7,6},{8,9},{9,8},{10,11... | collective-permute-start | bytes 122888 | tf_op jit(solution)/shard_map/ppermute | solution.py:530
  2.3 2.6 %collective-permute-start.1 = (bf16[160,128]{1,0:T(8,128)(2,1)S(1)}, bf16[160,128]{1,0:T(8,128)(2,1)S(1)}, u32[]{:S(2)}, u32[]{:S(2)}) collective-permute-start(bf16[160,128]{1,0:T(8,128)(2,1)S(1)} %get-tuple-element.65), channel_id=1, source_target_pairs={{0,4},{1,2},{2,1},{3,7},{4,0},{5,6},{6,5},{7,3},{8,12},{9,10},{10,... | collective-permute-start | bytes 122888 | tf_op jit(solution)/shard_map/ppermute | solution.py:531
  4.8 1.7 %shard_map.102 = (bf16[1152,384]{1,0:T(8,128)(2,1)S(1)}, bf16[9,384,128]{2,1,0:T(8,128)(2,1)S(1)}, f32[1,128]{1,0:T(1,128)S(1)}, bf16[27,96,96]{2,1,0:T(8,128)(2,1)S(1)}, bf16[27,96,96]{2,1,0:T(8,128)(2,1)S(1)}) custom-call(bf16[27,96,96]{2,1,0:T(8,128)(2,1)} %cw_far.1, bf16[27,96,96]{2,1,0:T(8,128)(2,1)} %dw_far.1, f32[1,96]{1,0:T(1,128)} %bitcast.10), custom_call_target="tpu_custom_call" | custom-call | tf_op jit(solution)/shard_map/pallas_call | solution.py:28
  6.6 0.0 collective-permute-done.core_ref
  6.6 0.2 collective-permute-done.1.side_ref
  6.8 0.1 shard_map.103
  6.9 0.2 collective-permute-start.2
  7.1 3.5 %collective-permute-start.3 = (bf16[240,128]{1,0:T(8,128)(2,1)S(1)}, bf16[240,128]{1,0:T(8,128)(2,1)S(1)}, u32[]{:S(2)}, u32[]{:S(2)}) collective-permute-start(bf16[240,128]{1,0:T(8,128)(2,1)S(1)} %get-tuple-element.74), channel_id=1, source_target_pairs={{0,4},{4,0},{8,12},{12,8},{16,20},{20,16},{24,28},{28,24},{1,5},{5... | collective-permute-start | bytes 184328 | tf_op jit(solution)/shard_map/ppermute | solution.py:558
  10.5 2.3 %shard_map.104 = (bf16[480,128]{1,0:T(8,128)(2,1)S(1)}, bf16[480,128]{1,0:T(8,128)(2,1)S(1)}, f32[384,128]{1,0:T(8,128)S(1)}, f32[1152,384]{1,0:T(8,128)S(1)}) custom-call(bf16[512,128]{1,0:T(8,128)(2,1)S(1)} %get-tuple-element.62.x_ref, bf16[128,128]{1,0:T(8,128)(2,1)S(1)} %get-tuple-element.63.u_ref, bf16[160,128]{1,0:T(8,128)(2,1)S(1)} %collective-permute-done.core_ref, ...), custom_call_target="tpu_custom_call" | custom-call | flops 5000000000 | bytes 4000000 | tf_op jit(solution)/shard_map/pallas_call | solution.py:28
  12.8 0.0 collective-permute-done.2.far_ref
  12.8 0.0 collective-permute-done.3.near_ref
  12.8 1.3 %shard_map.105 = (bf16[1984,128]{1,0:T(8,128)(2,1)S(1)}, bf16[320,128]{1,0:T(8,128)(2,1)S(1)}, bf16[320,128]{1,0:T(8,128)(2,1)S(1)}, f32[128,128]{1,0:T(8,128)S(...) custom-call(bf16[512,128]{1,0:T(8,128)(2,1)S(1)} %get-tuple-element.62.x_ref, ...), custom_call_target="tpu_custom_call" | custom-call | tf_op jit(solution)/shard_map/pallas_call | solution.py:28
  14.2 0.1 collective-permute-start.4
  14.2 0.4 shard_map.108
  14.7 0.6 %shard_map.106.keep_ref = f32[1984,128]{1,0:T(8,128)S(1)} custom-call(bf16[2,128,1152]{2,1,0:T(8,128)(2,1)S(1)} %get-tuple-element.88.win_ref, bf16[2,128,384]{2,1,0:T(8,128)(2,1)S(1)} %get-tuple-element.89.other_ref, f32[1152,384]{1,0:T(8,128)S(1)} %get-tuple-element.86.acc_ref), custom_call_target="tpu_custom_call" | custom-call | flops 2000000000 | bytes 4000000 | tf_op jit(solution)/shard_map/pallas_call | solution.py:28
  15.2 0.9 %collective-permute-done.4.got_ref = bf16[1984,128]{1,0:T(8,128)(2,1)S(1)} collective-permute-done((bf16[1984,128]{1,0:T(8,128)(2,1)S(1)}, bf16[1984,128]{1,0:T(8,128)(2,1)S(1)}, u32[]{:S(2)}, u32[]{:S(2)}) %collective-permute-start.4) | collective-permute-done | bytes 507936 | tf_op jit(solution)/shard_map/ppermute | solution.py:603
  16.1 0.1 shard_map.107
  16.2 1.0 %collective-permute-start.5 = (bf16[496,128]{1,0:T(8,128)(2,1)S(1)}, bf16[496,128]{1,0:T(8,128)(2,1)S(1)}, u32[]{:S(2)}, u32[]{:S(2)}) collective-permute-start(bf16[496,128]{1,0:T(8,128)(2,1)S(1)} %get-tuple-element.92), channel_id=1, source_target_pairs={{0,2},{1,5},{2,0},{3,7},{4,6},{5,1},{6,4},{7,3},{8,10},{9,13},{10,... | collective-permute-start | bytes 380936 | tf_op jit(solution)/shard_map/ppermute | solution.py:652
  17.2 2.4 %collective-permute-start.6 = (bf16[496,128]{1,0:T(8,128)(2,1)S(1)}, bf16[496,128]{1,0:T(8,128)(2,1)S(1)}, u32[]{:S(2)}, u32[]{:S(2)}) collective-permute-start(bf16[496,128]{1,0:T(8,128)(2,1)S(1)} %get-tuple-element.93), channel_id=1, source_target_pairs={{0,4},{1,3},{2,6},{3,1},{4,0},{5,7},{6,2},{7,5},{8,12},{9,11},{10,... | collective-permute-start | bytes 380936 | tf_op jit(solution)/shard_map/ppermute | solution.py:652
  19.6 0.5 %collective-permute-start.7 = (bf16[496,128]{1,0:T(8,128)(2,1)S(1)}, bf16[496,128]{1,0:T(8,128)(2,1)S(1)}, u32[]{:S(2)}, u32[]{:S(2)}) collective-permute-start(bf16[496,128]{1,0:T(8,128)(2,1)S(1)} %get-tuple-element.94), channel_id=1, source_target_pairs={{0,6},{1,7},{2,4},{3,5},{4,2},{5,3},{6,0},{7,1},{8,14},{9,15},{10,... | collective-permute-start | bytes 380936 | tf_op jit(solution)/shard_map/ppermute | solution.py:652
  20.1 1.7 %shard_map.109 = (bf16[64,96]{1,0:T(8,128)(2,1)}, bf16[512,96]{1,0:T(8,128)(2,1)}) custom-call(bf16[512,128]{1,0:T(8,128)(2,1)S(1)} %get-tuple-element.62.x_ref, bf16[128,128]{1,0:T(8,128)(2,1)S(1)} %get-tuple-element.63.u_ref, bf16[480,128]{1,0:T(8,128)(2,1)S(1)} %get-tuple-element.84.gpa_ref, bf16[320,128]{1,0:T(8,128)(2,1)S(1)} %get-tuple-element.95.gpb_ref, ...), custom_call_target="tpu_custom_call" | custom-call | flops 5000000000 | bytes 4000000 | tf_op jit(solution)/shard_map/pallas_call | solution.py:28
  21.8 0.0 collective-permute-done.5.a_ref
  21.8 1.2 %collective-permute-done.6.b_ref = bf16[496,128]{1,0:T(8,128)(2,1)S(1)} collective-permute-done((bf16[496,128]{1,0:T(8,128)(2,1)S(1)}, bf16[496,128]{1,0:T(8,128)(2,1)S(1)}, u32[]{:S(2)}, u32[]{:S(2)}) %collective-permute-start.6) | collective-permute-done | bytes 127008 | tf_op jit(solution)/shard_map/ppermute | solution.py:652
  23.0 2.8 %collective-permute-done.7.c_ref = bf16[496,128]{1,0:T(8,128)(2,1)S(1)} collective-permute-done((bf16[496,128]{1,0:T(8,128)(2,1)S(1)}, bf16[496,128]{1,0:T(8,128)(2,1)S(1)}, u32[]{:S(2)}, u32[]{:S(2)}) %collective-permute-start.7) | collective-permute-done | bytes 127008 | tf_op jit(solution)/shard_map/ppermute | solution.py:652
  25.8 0.1 shard_map.110
  25.8 2.2 %collective-permute-start.8 = (bf16[496,128]{1,0:T(8,128)(2,1)S(1)}, bf16[496,128]{1,0:T(8,128)(2,1)S(1)}, u32[]{:S(2)}, u32[]{:S(2)}) collective-permute-start(bf16[496,128]{1,0:T(8,128)(2,1)S(1)} %shard_map.110), channel_id=1, source_target_pairs={{0,8},{1,17},{2,10},{3,19},{4,12},{5,21},{6,14},{7,23},{8,0},{9,25... | collective-permute-start | bytes 380936 | tf_op jit(solution)/shard_map/ppermute | solution.py:670
  28.0 3.6 %collective-permute-done.8 = bf16[496,128]{1,0:T(8,128)(2,1)S(1)} collective-permute-done((bf16[496,128]{1,0:T(8,128)(2,1)S(1)}, bf16[496,128]{1,0:T(8,128)(2,1)S(1)}, u32[]{:S(2)}, u32[]{:S(2)}) %collective-permute-start.8) | collective-permute-done | bytes 127008 | tf_op jit(solution)/shard_map/ppermute | solution.py:670
  31.7 2.4 %collective-permute-start.9 = (bf16[496,128]{1,0:T(8,128)(2,1)S(1)}, bf16[496,128]{1,0:T(8,128)(2,1)S(1)}, u32[]{:S(2)}, u32[]{:S(2)}) collective-permute-start(bf16[496,128]{1,0:T(8,128)(2,1)S(1)} %add_convert_fusion.1), channel_id=1, source_target_pairs={{0,16},{1,9},{2,18},{3,11},{4,20},{5,13},{6,22},{7,15},{8,24},{9,1... | collective-permute-start | bytes 380936 | tf_op jit(solution)/shard_map/ppermute | solution.py:670
  34.1 3.5 %collective-permute-done.9 = bf16[496,128]{1,0:T(8,128)(2,1)S(1)} collective-permute-done((bf16[496,128]{1,0:T(8,128)(2,1)S(1)}, bf16[496,128]{1,0:T(8,128)(2,1)S(1)}, u32[]{:S(2)}, u32[]{:S(2)}) %collective-permute-start.9) | collective-permute-done | bytes 127008 | tf_op jit(solution)/shard_map/ppermute | solution.py:670
  37.6 1.1 %collective-permute-start.11 = (bf16[496,128]{1,0:T(8,128)(2,1)S(1)}, bf16[496,128]{1,0:T(8,128)(2,1)S(1)}, u32[]{:S(2)}, u32[]{:S(2)}) collective-permute-start(bf16[496,128]{1,0:T(8,128)(2,1)S(1)} %add_convert_fusion.refs_0_), channel_id=1, source_target_pairs={{0,2},{1,5},{2,0},{3,7},{4,6},{5,1},{6,4},{7,3},{8,10},{9,13},{10,... | collective-permute-start | bytes 380936 | tf_op jit(solution)/shard_map/ppermute | solution.py:652
  38.7 2.2 %collective-permute-start.13 = (bf16[496,128]{1,0:T(8,128)(2,1)S(1)}, bf16[496,128]{1,0:T(8,128)(2,1)S(1)}, u32[]{:S(2)}, u32[]{:S(2)}) collective-permute-start(bf16[496,128]{1,0:T(8,128)(2,1)S(1)} %add_convert_fusion.refs_0_), channel_id=1, source_target_pairs={{0,4},{1,3},{2,6},{3,1},{4,0},{5,7},{6,2},{7,5},{8,12},{9,11},{10,... | collective-permute-start | bytes 380936 | tf_op jit(solution)/shard_map/ppermute | solution.py:652
  41.0 0.4 collective-permute-start.14
  41.3 1.5 %collective-permute-done.11.refs_1_ = bf16[496,128]{1,0:T(8,128)(2,1)S(1)} collective-permute-done((bf16[496,128]{1,0:T(8,128)(2,1)S(1)}, bf16[496,128]{1,0:T(8,128)(2,1)S(1)}, u32[]{:S(2)}, u32[]{:S(2)}) %collective-permute-start.11) | collective-permute-done | bytes 127008 | tf_op jit(solution)/shard_map/ppermute | solution.py:652
  42.8 0.0 collective-permute-start.12
  42.8 0.5 %collective-permute-start.10 = (bf16[496,128]{1,0:T(8,128)(2,1)S(1)}, bf16[496,128]{1,0:T(8,128)(2,1)S(1)}, u32[]{:S(2)}, u32[]{:S(2)}) collective-permute-start(bf16[496,128]{1,0:T(8,128)(2,1)S(1)} %add_convert_fusion.refs_0_), channel_id=1, source_target_pairs={{0,1},{1,0},{2,3},{3,2},{4,5},{5,4},{6,7},{7,6},{8,9},{9,8},{10,11... | collective-permute-start | bytes 380936 | tf_op jit(solution)/shard_map/ppermute | solution.py:674
  43.3 0.5 %collective-permute-done.13.refs_2_ = bf16[496,128]{1,0:T(8,128)(2,1)S(1)} collective-permute-done((bf16[496,128]{1,0:T(8,128)(2,1)S(1)}, bf16[496,128]{1,0:T(8,128)(2,1)S(1)}, u32[]{:S(2)}, u32[]{:S(2)}) %collective-permute-start.13) | collective-permute-done | bytes 127008 | tf_op jit(solution)/shard_map/ppermute | solution.py:652
  43.9 0.0 collective-permute-start.15
  43.9 2.9 %collective-permute-done.14.refs_3_ = bf16[496,128]{1,0:T(8,128)(2,1)S(1)} collective-permute-done((bf16[496,128]{1,0:T(8,128)(2,1)S(1)}, bf16[496,128]{1,0:T(8,128)(2,1)S(1)}, u32[]{:S(2)}, u32[]{:S(2)}) %collective-permute-start.14) | collective-permute-done | bytes 127008 | tf_op jit(solution)/shard_map/ppermute | solution.py:652
  46.8 0.0 collective-permute-start.16
  46.8 0.4 shard_map.111
  47.2 0.0 collective-permute-done.12.refs_1_
  47.2 0.0 collective-permute-done.10.refs_0_
  47.2 0.0 collective-permute-done.15.refs_2_
  47.2 0.9 %collective-permute-done.16.refs_3_ = bf16[496,128]{1,0:T(8,128)(2,1)S(1)} collective-permute-done((bf16[496,128]{1,0:T(8,128)(2,1)S(1)}, bf16[496,128]{1,0:T(8,128)(2,1)S(1)}, u32[]{:S(2)}, u32[]{:S(2)}) %collective-permute-start.16) | collective-permute-done | bytes 127008 | tf_op jit(solution)/shard_map/ppermute | solution.py:674
  48.1 1.6 %shard_map.112 = (f32[27,96,96]{2,1,0:T(8,128)}, f32[27,96,96]{2,1,0:T(8,128)}, f32[1,96]{1,0:T(1,128)}) custom-call(bf16[496,128]{1,0:T(8,128)(2,1)S(1)} %collective-permute-done.10.refs_0_, bf16[496,128]{1,0:T(8,128)(2,1)S(1)} %collective-permute-done.12.refs_1_, bf16[496,128]{1,0:T(8,128)(2,1)S(1)} %collective-permute-done.15.refs_2_, ...), custom_call_target="tpu_custom_call" | custom-call | tf_op jit(solution)/shard_map/pallas_call | solution.py:28
  (2 shorter events, 0.1 us)
Async XLA Ops:
  1.7 4.8 %collective-permute-start = (bf16[160,128]{1,0:T(8,128)(2,1)S(1)}, bf16[160,128]{1,0:T(8,128)(2,1)S(1)}, u32[]{:S(2)}, u32[]{:S(2)}) collective-permute-start(bf16[160,128]{1,0:T(8,128)(2,1)S(1)} %get-tuple-element.64), channel_id=1, source_target_pairs={{0,1},{1,0},{2,3},{3,2},{4,5},{5,4},{6,7},{7,6},{8,9},{9,8},{10,11... | collective-permute-start | bytes 122888 | tf_op jit(solution)/shard_map/ppermute | solution.py:530
  2.3 4.5 %collective-permute-start.1 = (bf16[160,128]{1,0:T(8,128)(2,1)S(1)}, bf16[160,128]{1,0:T(8,128)(2,1)S(1)}, u32[]{:S(2)}, u32[]{:S(2)}) collective-permute-start(bf16[160,128]{1,0:T(8,128)(2,1)S(1)} %get-tuple-element.65), channel_id=1, source_target_pairs={{0,4},{1,2},{2,1},{3,7},{4,0},{5,6},{6,5},{7,3},{8,12},{9,10},{10,... | collective-permute-start | bytes 122888 | tf_op jit(solution)/shard_map/ppermute | solution.py:531
  6.9 5.9 %collective-permute-start.2 = (bf16[240,128]{1,0:T(8,128)(2,1)S(1)}, bf16[240,128]{1,0:T(8,128)(2,1)S(1)}, u32[]{:S(2)}, u32[]{:S(2)}) collective-permute-start(bf16[240,128]{1,0:T(8,128)(2,1)S(1)} %get-tuple-element.73), channel_id=1, source_target_pairs={{0,1},{1,0},{2,3},{3,2},{4,8},{5,9},{6,10},{7,11},{8,4},{9,5},{10,... | collective-permute-start | bytes 184328 | tf_op jit(solution)/shard_map/ppermute | solution.py:559
  7.1 5.7 %collective-permute-start.3 = (bf16[240,128]{1,0:T(8,128)(2,1)S(1)}, bf16[240,128]{1,0:T(8,128)(2,1)S(1)}, u32[]{:S(2)}, u32[]{:S(2)}) collective-permute-start(bf16[240,128]{1,0:T(8,128)(2,1)S(1)} %get-tuple-element.74), channel_id=1, source_target_pairs={{0,4},{4,0},{8,12},{12,8},{16,20},{20,16},{24,28},{28,24},{1,5},{5... | collective-permute-start | bytes 184328 | tf_op jit(solution)/shard_map/ppermute | solution.py:558
  14.2 2.0 %collective-permute-start.4 = (bf16[1984,128]{1,0:T(8,128)(2,1)S(1)}, bf16[1984,128]{1,0:T(8,128)(2,1)S(1)}, u32[]{:S(2)}, u32[]{:S(2)}) collective-permute-start(bf16[1984,128]{1,0:T(8,128)(2,1)S(1)} %get-tuple-element.87), channel_id=1, source_target_pairs={{0,1},{1,0},{2,3},{3,2},{4,5},{5,4},{6,7},{7,6},{8,9},{9,8},{10,11... | collective-permute-start | bytes 1523720 | tf_op jit(solution)/shard_map/ppermute | solution.py:603
  16.2 5.6 %collective-permute-start.5 = (bf16[496,128]{1,0:T(8,128)(2,1)S(1)}, bf16[496,128]{1,0:T(8,128)(2,1)S(1)}, u32[]{:S(2)}, u32[]{:S(2)}) collective-permute-start(bf16[496,128]{1,0:T(8,128)(2,1)S(1)} %get-tuple-element.92), channel_id=1, source_target_pairs={{0,2},{1,5},{2,0},{3,7},{4,6},{5,1},{6,4},{7,3},{8,10},{9,13},{10,... | collective-permute-start | bytes 380936 | tf_op jit(solution)/shard_map/ppermute | solution.py:652
  17.2 5.8 %collective-permute-start.6 = (bf16[496,128]{1,0:T(8,128)(2,1)S(1)}, bf16[496,128]{1,0:T(8,128)(2,1)S(1)}, u32[]{:S(2)}, u32[]{:S(2)}) collective-permute-start(bf16[496,128]{1,0:T(8,128)(2,1)S(1)} %get-tuple-element.93), channel_id=1, source_target_pairs={{0,4},{1,3},{2,6},{3,1},{4,0},{5,7},{6,2},{7,5},{8,12},{9,11},{10,... | collective-permute-start | bytes 380936 | tf_op jit(solution)/shard_map/ppermute | solution.py:652
  19.6 6.1 %collective-permute-start.7 = (bf16[496,128]{1,0:T(8,128)(2,1)S(1)}, bf16[496,128]{1,0:T(8,128)(2,1)S(1)}, u32[]{:S(2)}, u32[]{:S(2)}) collective-permute-start(bf16[496,128]{1,0:T(8,128)(2,1)S(1)} %get-tuple-element.94), channel_id=1, source_target_pairs={{0,6},{1,7},{2,4},{3,5},{4,2},{5,3},{6,0},{7,1},{8,14},{9,15},{10,... | collective-permute-start | bytes 380936 | tf_op jit(solution)/shard_map/ppermute | solution.py:652
  25.8 5.8 %collective-permute-start.8 = (bf16[496,128]{1,0:T(8,128)(2,1)S(1)}, bf16[496,128]{1,0:T(8,128)(2,1)S(1)}, u32[]{:S(2)}, u32[]{:S(2)}) collective-permute-start(bf16[496,128]{1,0:T(8,128)(2,1)S(1)} %shard_map.110), channel_id=1, source_target_pairs={{0,8},{1,17},{2,10},{3,19},{4,12},{5,21},{6,14},{7,23},{8,0},{9,25... | collective-permute-start | bytes 380936 | tf_op jit(solution)/shard_map/ppermute | solution.py:670
  31.7 5.9 %collective-permute-start.9 = (bf16[496,128]{1,0:T(8,128)(2,1)S(1)}, bf16[496,128]{1,0:T(8,128)(2,1)S(1)}, u32[]{:S(2)}, u32[]{:S(2)}) collective-permute-start(bf16[496,128]{1,0:T(8,128)(2,1)S(1)} %add_convert_fusion.1), channel_id=1, source_target_pairs={{0,16},{1,9},{2,18},{3,11},{4,20},{5,13},{6,22},{7,15},{8,24},{9,1... | collective-permute-start | bytes 380936 | tf_op jit(solution)/shard_map/ppermute | solution.py:670
  37.6 5.2 %collective-permute-start.11 = (bf16[496,128]{1,0:T(8,128)(2,1)S(1)}, bf16[496,128]{1,0:T(8,128)(2,1)S(1)}, u32[]{:S(2)}, u32[]{:S(2)}) collective-permute-start(bf16[496,128]{1,0:T(8,128)(2,1)S(1)} %add_convert_fusion.refs_0_), channel_id=1, source_target_pairs={{0,2},{1,5},{2,0},{3,7},{4,6},{5,1},{6,4},{7,3},{8,10},{9,13},{10,... | collective-permute-start | bytes 380936 | tf_op jit(solution)/shard_map/ppermute | solution.py:652
  38.7 5.1 %collective-permute-start.13 = (bf16[496,128]{1,0:T(8,128)(2,1)S(1)}, bf16[496,128]{1,0:T(8,128)(2,1)S(1)}, u32[]{:S(2)}, u32[]{:S(2)}) collective-permute-start(bf16[496,128]{1,0:T(8,128)(2,1)S(1)} %add_convert_fusion.refs_0_), channel_id=1, source_target_pairs={{0,4},{1,3},{2,6},{3,1},{4,0},{5,7},{6,2},{7,5},{8,12},{9,11},{10,... | collective-permute-start | bytes 380936 | tf_op jit(solution)/shard_map/ppermute | solution.py:652
  41.0 5.8 %collective-permute-start.14 = (bf16[496,128]{1,0:T(8,128)(2,1)S(1)}, bf16[496,128]{1,0:T(8,128)(2,1)S(1)}, u32[]{:S(2)}, u32[]{:S(2)}) collective-permute-start(bf16[496,128]{1,0:T(8,128)(2,1)S(1)} %add_convert_fusion.refs_0_), channel_id=1, source_target_pairs={{0,6},{1,7},{2,4},{3,5},{4,2},{5,3},{6,0},{7,1},{8,14},{9,15},{10,... | collective-permute-start | bytes 380936 | tf_op jit(solution)/shard_map/ppermute | solution.py:652
  42.8 4.4 %collective-permute-start.12 = (bf16[496,128]{1,0:T(8,128)(2,1)S(1)}, bf16[496,128]{1,0:T(8,128)(2,1)S(1)}, u32[]{:S(2)}, u32[]{:S(2)}) collective-permute-start(bf16[496,128]{1,0:T(8,128)(2,1)S(1)} %collective-permute-done.11.refs_1_), channel_id=1, source_target_pairs={{0,1},{1,0},{2,3},{3,2},{4,5},{5,4},{6,7},{7,6},{8,9},{9,8},{10,11... | collective-permute-start | bytes 380936 | tf_op jit(solution)/shard_map/ppermute | solution.py:674
  42.8 4.4 %collective-permute-start.10 = (bf16[496,128]{1,0:T(8,128)(2,1)S(1)}, bf16[496,128]{1,0:T(8,128)(2,1)S(1)}, u32[]{:S(2)}, u32[]{:S(2)}) collective-permute-start(bf16[496,128]{1,0:T(8,128)(2,1)S(1)} %add_convert_fusion.refs_0_), channel_id=1, source_target_pairs={{0,1},{1,0},{2,3},{3,2},{4,5},{5,4},{6,7},{7,6},{8,9},{9,8},{10,11... | collective-permute-start | bytes 380936 | tf_op jit(solution)/shard_map/ppermute | solution.py:674
  43.9 3.4 %collective-permute-start.15 = (bf16[496,128]{1,0:T(8,128)(2,1)S(1)}, bf16[496,128]{1,0:T(8,128)(2,1)S(1)}, u32[]{:S(2)}, u32[]{:S(2)}) collective-permute-start(bf16[496,128]{1,0:T(8,128)(2,1)S(1)} %collective-permute-done.13.refs_2_), channel_id=1, source_target_pairs={{0,1},{1,0},{2,3},{3,2},{4,5},{5,4},{6,7},{7,6},{8,9},{9,8},{10,11... | collective-permute-start | bytes 380936 | tf_op jit(solution)/shard_map/ppermute | solution.py:674
  46.8 1.3 %collective-permute-start.16 = (bf16[496,128]{1,0:T(8,128)(2,1)S(1)}, bf16[496,128]{1,0:T(8,128)(2,1)S(1)}, u32[]{:S(2)}, u32[]{:S(2)}) collective-permute-start(bf16[496,128]{1,0:T(8,128)(2,1)S(1)} %collective-permute-done.14.refs_3_), channel_id=1, source_target_pairs={{0,1},{1,0},{2,3},{3,2},{4,5},{5,4},{6,7},{7,6},{8,9},{9,8},{10,11... | collective-permute-start | bytes 380936 | tf_op jit(solution)/shard_map/ppermute | solution.py:674
